TPU v7x, 256 devices: a whole 4x4x8 slice. The times are simulated.
256 devices in a mesh: sec: 64 (over y, z, core), reg: 4 (over x).
Axes of the slice: x: 4, y: 4, z: 8, core: 2. Of those that a mesh axis runs over, the one named last changes fastest.
Arguments:
- start_params: float32 [64, 4, 20, 128], P('sec', 'reg'), may hold values from -3 to 3
- right_side: float32 [64, 4, 20, 128], P('sec', 'reg'), may hold values from -40 to 40
- prior: float32 [64, 4, 20, 128], P('sec', 'reg'), may hold values from 0.1 to 1
- matches: bfloat16 [64, 4, 640, 4, 256], P('sec', 'reg'), may hold values from -1 to 1
- pair_first: int32 [64, 4, 640], P('sec', 'reg'), may hold values from 0 to 127, as said below
- pair_second: int32 [64, 4, 640], P('sec', 'reg'), may hold values from 0 to 415, as said below
- match_counts: int32 [64, 4, 640], P('sec', 'reg'), may hold values from 0 to 256, as said below
- send_lists: int32 [64, 4, 2, 16], P('sec', 'reg'), may hold values from 0 to 127, as said below
Outputs:
- solution: float32 [64, 4, 20, 128], P('sec', 'reg')
- residual: float32 [64, 4, 20, 128], P('sec', 'reg')
Inputs may be any that keep to these rules, and one draw needn't show every extreme that they name: Each tile is pair_first of exactly five pairs of its device, in a drawn order. `pair_second`: names a column of the extended field; blocks of neighbours outside the grid are never named; a pair with match count 0 names its own tile. `match_counts`: 0 marks an absent pair; every device has a pair with exactly 256 matches. `send_lists`: row 0 holds the tiles whose coefficients a region lends to the region below it, row 1 to the region above; each row has 16 distinct tiles and the rows are disjoint.
All inputs are finite; a program needn't handle non-finite values.
Results may differ from a plain program's by a relative error of at most 0.0003.
Values sent between devices are 32-bit elements; how exact they have to be, the bound alone decides.
A program may use at most 64 MiB of HBM per device.

v0:
```python
import math
import jax
import jax.numpy as jnp
from jax import lax
from jax.sharding import PartitionSpec as P

FULL_PRECISION = lax.Precision.HIGHEST


def shifted(array, axis, by):
    length = lax.axis_size(axis)
    pairs = [(i, i + by) for i in range(length) if 0 <= i + by < length]
    return lax.ppermute(array, axis, pairs)


def padded_2(array, sides, width):
    for axis, dim in sides:
        size, length = (lax.axis_size(axis), array.shape[dim])
        up = [(i, (i + 1) % size) for i in range(size - 1)]
        down = [(j, i) for i, j in up]
        last = lax.slice_in_dim(array, length - width, length, axis=dim)
        first = lax.slice_in_dim(array, 0, width, axis=dim)
        before = lax.ppermute(last, axis, up)
        after = lax.ppermute(first, axis, down)
        array = jnp.concatenate([before, array, after], axis=dim)
    return array


def monomials(across, upward):
    constant = jnp.ones_like(across)
    square_a = across * across
    square_b = upward * upward
    mixed = across * upward
    return jnp.stack(
        [
            constant,
            across,
            upward,
            square_a,
            mixed,
            square_b,
            square_a * across,
            square_a * upward,
            square_b * across,
            square_b * upward,
        ]
    )


def match_bases(count_blk, match_blk):
    points = match_blk.astype(jnp.float32)
    slots = points.shape[-1]
    basis_a = monomials(points[:, 0], points[:, 1])
    basis_b = monomials(points[:, 2], points[:, 3])
    weights = jnp.where(jnp.arange(slots)[None, :] < count_blk[:, None], 2.0 / slots, 0.0).astype(
        jnp.float32
    )
    return (basis_a, basis_b, weights)


def block_terms(extended, first_blk, second_blk, count_blk, match_blk):
    width = first_blk.shape[0]
    basis_a, basis_b, weights = match_bases(count_blk, match_blk)
    own = jnp.take(extended, first_blk, axis=1).reshape(2, 10, width)
    other = jnp.take(extended, second_blk, axis=1).reshape(2, 10, width)
    mismatch = (
        jnp.einsum("mpk,cmp->cpk", basis_a, own, precision=FULL_PRECISION)
        - jnp.einsum("mpk,cmp->cpk", basis_b, other, precision=FULL_PRECISION)
    ) * weights[None]
    to_own = jnp.einsum("mpk,cpk->cmp", basis_a, mismatch, precision=FULL_PRECISION).reshape(
        20, width
    )
    to_other = -jnp.einsum("mpk,cpk->cmp", basis_b, mismatch, precision=FULL_PRECISION).reshape(
        20, width
    )
    return (to_own, to_other)


def split_blocks(first, second, counts, matches):
    pairs = first.shape[0]
    block = math.gcd(pairs, 512)
    blocks = pairs // block
    slots = matches.shape[-1]
    return (
        first.reshape(blocks, block),
        second.reshape(blocks, block),
        counts.reshape(blocks, block),
        matches.reshape(blocks, block, 4, slots),
    )


def extend(params, send_lists):
    arrived = params
    taken = []
    for hop_index in range(2):
        arrived = shifted(arrived, "sec", 1)
        taken.append(arrived)
    near_params, far_params = (taken[0], taken[1])
    faces = jnp.stack(
        [jnp.take(params, send_lists[0], axis=1), jnp.take(params, send_lists[1], axis=1)]
    )
    padded = padded_2(faces, (("reg", 0),), 1)
    return jnp.concatenate([params, near_params, far_params, padded[0], padded[3]], axis=1)


def fold_back(products, tiles, rows, send_lists):
    local = products[:, :tiles]
    near_part = products[:, tiles : 2 * tiles]
    far_part = products[:, 2 * tiles : 3 * tiles]
    outgoing = far_part
    arrived = far_part
    for hop_index in range(2):
        arrived = shifted(outgoing, "sec", -1)
        outgoing = near_part + arrived
    local = local + arrived
    faces = jnp.stack([products[:, 3 * tiles : 3 * tiles + rows], products[:, 3 * tiles + rows :]])
    padded = padded_2(faces, (("reg", 0),), 1)
    local = local.at[:, send_lists[0]].add(padded[0])
    return local.at[:, send_lists[1]].add(padded[3])


def apply_normal(params, prior, first, second, counts, matches, send_lists):
    tiles = params.shape[1]
    rows = send_lists.shape[1]
    pairs = first.shape[0]
    extended = extend(params, send_lists)
    pieces = split_blocks(first, second, counts, matches)
    to_own, to_other = lax.map(
        lambda items: block_terms(extended, items[0], items[1], items[2], items[3]), pieces
    )
    to_own = jnp.moveaxis(to_own, 0, 1).reshape(20, pairs)
    to_other = jnp.moveaxis(to_other, 0, 1).reshape(20, pairs)
    products = jnp.zeros((20, extended.shape[1]), jnp.float32)
    products = products.at[:, first].add(to_own).at[:, second].add(to_other)
    return fold_back(products, tiles, rows, send_lists) + prior * params


def global_dot(value):
    return lax.psum(value, ("sec", "reg"))


def on_device(
    start_params, right_side, prior, matches, pair_first, pair_second, match_counts, send_lists
):
    params_start = start_params[0, 0]
    target = right_side[0, 0]
    damping = prior[0, 0]
    first = pair_first[0, 0]
    second = pair_second[0, 0]
    counts = match_counts[0, 0]
    points = matches[0, 0]
    border = send_lists[0, 0]

    def normal(field):
        return apply_normal(field, damping, first, second, counts, points, border)

    solution = params_start
    residual = target - normal(params_start)
    direction = residual
    norm_now = global_dot(jnp.sum(residual * residual))
    image = normal(direction)
    alpha = norm_now / global_dot(jnp.sum(direction * image))
    solution = solution + alpha * direction
    residual = residual - alpha * image
    return (solution[None, None], residual[None, None])


def solution(mesh):
    return jax.shard_map(
        on_device,
        mesh=mesh,
        in_specs=(
            P("sec", "reg", None, None),
            P("sec", "reg", None, None),
            P("sec", "reg", None, None),
            P("sec", "reg", None, None, None),
            P("sec", "reg", None),
            P("sec", "reg", None),
            P("sec", "reg", None),
            P("sec", "reg", None, None),
        ),
        out_specs=(P("sec", "reg", None, None), P("sec", "reg", None, None)),
        check_vma=False,
    )
```

profile of v0, /device:TPU:1, one launch (start us, length us, event | category | flops | bytes accessed | tf_op | source)
XLA Modules:
  0.0 497.0 jit_solution(6133939188612458602)
XLA Ops:
  1.4 4.9 collective-permute-start
  23.0 152.0 %while.24 = (s32[]{:T(128)}, f32[5,20,128]{2,1,0:T(8,128)}, f32[5,20,128]{2,1,0:T(8,128)}, s32[5,128]{1,0:T(8,128)S(1)}, f32[20,416]{0,1:T(8,128)}, /*index=5*/b...) while((s32[]{:T(128)}, f32[5,20,128]{2,1,0:T(8,128)}, ...), condition=%wide.region_1.4_spmd, body=%wide.region_0.3_spmd.sunk | while | flops 32287744 | bytes 16952436 | solution.py:128
  27.2 4.8 stack.53
  32.7 5.4 %stack.52 = f32[10,128,256]{2,0,1:T(8,128)} concatenate(f32[1,128,256]{2,0,1:T(1,128)S(1)} %broadcast.300, f32[1,128,256]{2,0,1:T(1,128)} %get-tuple-element.348, f32[1,128,256]{2,0,1:T(1,128)} %get-tuple-element.349, f32[1,128,256]{2,0,1:T(1,128)S(1)} %get-tuple-element.350, f32[1,128,256]{2,0,1:T(1,128)S(1)} %get-tuple-element.351, f32[1,128,256]{2,0,1:T(1,128)S(1)} %get-tuple-element.352, ...), dimensions={0} | concatenate | bytes 2621440 | tf_op jit(solution)/shard_map/while/body/eval_jaxpr/stack | solution.py:34
  57.6 4.8 stack.53
  63.1 5.4 %stack.52 = f32[10,128,256]{2,0,1:T(8,128)} concatenate(f32[1,128,256]{2,0,1:T(1,128)S(1)} %broadcast.300, f32[1,128,256]{2,0,1:T(1,128)} %get-tuple-element.348, f32[1,128,256]{2,0,1:T(1,128)} %get-tuple-element.349, f32[1,128,256]{2,0,1:T(1,128)S(1)} %get-tuple-element.350, f32[1,128,256]{2,0,1:T(1,128)S(1)} %get-tuple-element.351, f32[1,128,256]{2,0,1:T(1,128)S(1)} %get-tuple-element.352, ...), dimensions={0} | concatenate | bytes 2621440 | tf_op jit(solution)/shard_map/while/body/eval_jaxpr/stack | solution.py:34
  87.9 4.8 stack.53
  93.5 5.4 %stack.52 = f32[10,128,256]{2,0,1:T(8,128)} concatenate(f32[1,128,256]{2,0,1:T(1,128)S(1)} %broadcast.300, f32[1,128,256]{2,0,1:T(1,128)} %get-tuple-element.348, f32[1,128,256]{2,0,1:T(1,128)} %get-tuple-element.349, f32[1,128,256]{2,0,1:T(1,128)S(1)} %get-tuple-element.350, f32[1,128,256]{2,0,1:T(1,128)S(1)} %get-tuple-element.351, f32[1,128,256]{2,0,1:T(1,128)S(1)} %get-tuple-element.352, ...), dimensions={0} | concatenate | bytes 2621440 | tf_op jit(solution)/shard_map/while/body/eval_jaxpr/stack | solution.py:34
  118.3 4.8 stack.53
  123.9 5.4 %stack.52 = f32[10,128,256]{2,0,1:T(8,128)} concatenate(f32[1,128,256]{2,0,1:T(1,128)S(1)} %broadcast.300, f32[1,128,256]{2,0,1:T(1,128)} %get-tuple-element.348, f32[1,128,256]{2,0,1:T(1,128)} %get-tuple-element.349, f32[1,128,256]{2,0,1:T(1,128)S(1)} %get-tuple-element.350, f32[1,128,256]{2,0,1:T(1,128)S(1)} %get-tuple-element.351, f32[1,128,256]{2,0,1:T(1,128)S(1)} %get-tuple-element.352, ...), dimensions={0} | concatenate | bytes 2621440 | tf_op jit(solution)/shard_map/while/body/eval_jaxpr/stack | solution.py:34
  154.3 5.4 %stack.52 = f32[10,128,256]{2,0,1:T(8,128)} concatenate(f32[1,128,256]{2,0,1:T(1,128)S(1)} %broadcast.300, f32[1,128,256]{2,0,1:T(1,128)} %get-tuple-element.348, f32[1,128,256]{2,0,1:T(1,128)} %get-tuple-element.349, f32[1,128,256]{2,0,1:T(1,128)S(1)} %get-tuple-element.350, f32[1,128,256]{2,0,1:T(1,128)S(1)} %get-tuple-element.351, f32[1,128,256]{2,0,1:T(1,128)S(1)} %get-tuple-element.352, ...), dimensions={0} | concatenate | bytes 2621440 | tf_op jit(solution)/shard_map/while/body/eval_jaxpr/stack | solution.py:34
  177.2 6.4 %scatter_custom_fusion = f32[20,416]{0,1:T(8,128)S(1)} fusion(s32[640]{0:T(1024)} %fusion.40, f32[640,20]{1,0:T(8,128)S(1)} %copy.78, f32[]{:T(128)} %constant.56.clone.1), kind=kCustom, calls=%fused_computation.104 | custom fusion | flops 12800 | bytes 33792 | tf_op jit(solution)/shard_map/scatter-add | solution.py:134
  183.6 6.1 %scatter_fusion = f32[20,416]{0,1:T(8,128)S(1)} fusion(f32[20,416]{0,1:T(8,128)S(1)} %scatter_custom_fusion, s32[640]{0:T(1024)S(1)} %fusion.41, f32[640,20]{1,0:T(8,128)S(1)} %copy.80), kind=kCustom, calls=%fused_computation.9 | custom fusion | flops 12800 | bytes 156160 | tf_op jit(solution)/shard_map/scatter-add | solution.py:134
  206.6 5.1 %collective-permute-start.8 = (f32[20,128]{0,1:T(8,128)S(1)}, f32[20,128]{0,1:T(8,128)S(1)}, u32[]{:S(2)}, u32[]{:S(2)}) collective-permute-start(f32[20,128]{0,1:T(8,128)S(1)} %bitcast_subtract_fusion), channel_id=1, source_target_pairs={{0,4},{4,8},{8,12},{12,16},{16,20},{20,24},{24,28},{28,32},{32,36}... | collective-permute-start | bytes 30728 | tf_op jit(solution)/shard_map/ppermute | solution.py:13
  225.3 152.0 %while.25 = (s32[]{:T(128)}, f32[5,20,128]{2,1,0:T(8,128)}, f32[5,20,128]{2,1,0:T(8,128)}, s32[5,128]{1,0:T(8,128)S(1)}, f32[20,416]{0,1:T(8,128)}, /*index=5*/b...) while((s32[]{:T(128)}, f32[5,20,128]{2,1,0:T(8,128)}, ...), condition=%wide.region_9.12_spmd, body=%wide.region_8.11_spmd.sunk | while | flops 32287744 | bytes 16952436 | solution.py:128
  235.1 5.4 %stack.70 = f32[10,128,256]{2,0,1:T(8,128)} concatenate(f32[1,128,256]{2,0,1:T(1,128)S(1)} %broadcast.309, f32[1,128,256]{2,0,1:T(1,128)} %get-tuple-element.377, f32[1,128,256]{2,0,1:T(1,128)} %get-tuple-element.378, f32[1,128,256]{2,0,1:T(1,128)S(1)} %get-tuple-element.379, f32[1,128,256]{2,0,1:T(1,128)S(1)} %get-tuple-element.380, f32[1,128,256]{2,0,1:T(1,128)S(1)} %get-tuple-element.381, ...), dimensions={0} | concatenate | bytes 2621440 | tf_op jit(solution)/shard_map/while/body/eval_jaxpr/stack | solution.py:34
  259.9 4.8 stack.71
  265.5 5.4 %stack.70 = f32[10,128,256]{2,0,1:T(8,128)} concatenate(f32[1,128,256]{2,0,1:T(1,128)S(1)} %broadcast.309, f32[1,128,256]{2,0,1:T(1,128)} %get-tuple-element.377, f32[1,128,256]{2,0,1:T(1,128)} %get-tuple-element.378, f32[1,128,256]{2,0,1:T(1,128)S(1)} %get-tuple-element.379, f32[1,128,256]{2,0,1:T(1,128)S(1)} %get-tuple-element.380, f32[1,128,256]{2,0,1:T(1,128)S(1)} %get-tuple-element.381, ...), dimensions={0} | concatenate | bytes 2621440 | tf_op jit(solution)/shard_map/while/body/eval_jaxpr/stack | solution.py:34
  295.9 5.4 %stack.70 = f32[10,128,256]{2,0,1:T(8,128)} concatenate(f32[1,128,256]{2,0,1:T(1,128)S(1)} %broadcast.309, f32[1,128,256]{2,0,1:T(1,128)} %get-tuple-element.377, f32[1,128,256]{2,0,1:T(1,128)} %get-tuple-element.378, f32[1,128,256]{2,0,1:T(1,128)S(1)} %get-tuple-element.379, f32[1,128,256]{2,0,1:T(1,128)S(1)} %get-tuple-element.380, f32[1,128,256]{2,0,1:T(1,128)S(1)} %get-tuple-element.381, ...), dimensions={0} | concatenate | bytes 2621440 | tf_op jit(solution)/shard_map/while/body/eval_jaxpr/stack | solution.py:34
  326.2 5.4 %stack.70 = f32[10,128,256]{2,0,1:T(8,128)} concatenate(f32[1,128,256]{2,0,1:T(1,128)S(1)} %broadcast.309, f32[1,128,256]{2,0,1:T(1,128)} %get-tuple-element.377, f32[1,128,256]{2,0,1:T(1,128)} %get-tuple-element.378, f32[1,128,256]{2,0,1:T(1,128)S(1)} %get-tuple-element.379, f32[1,128,256]{2,0,1:T(1,128)S(1)} %get-tuple-element.380, f32[1,128,256]{2,0,1:T(1,128)S(1)} %get-tuple-element.381, ...), dimensions={0} | concatenate | bytes 2621440 | tf_op jit(solution)/shard_map/while/body/eval_jaxpr/stack | solution.py:34
  356.6 5.4 %stack.70 = f32[10,128,256]{2,0,1:T(8,128)} concatenate(f32[1,128,256]{2,0,1:T(1,128)S(1)} %broadcast.309, f32[1,128,256]{2,0,1:T(1,128)} %get-tuple-element.377, f32[1,128,256]{2,0,1:T(1,128)} %get-tuple-element.378, f32[1,128,256]{2,0,1:T(1,128)S(1)} %get-tuple-element.379, f32[1,128,256]{2,0,1:T(1,128)S(1)} %get-tuple-element.380, f32[1,128,256]{2,0,1:T(1,128)S(1)} %get-tuple-element.381, ...), dimensions={0} | concatenate | bytes 2621440 | tf_op jit(solution)/shard_map/while/body/eval_jaxpr/stack | solution.py:34
  379.5 6.4 %scatter_custom_fusion.4 = f32[20,416]{0,1:T(8,128)S(1)} fusion(s32[640]{0:T(1024)} %fusion.40, f32[640,20]{1,0:T(8,128)S(1)} %copy.89, f32[]{:T(128)} %constant.56.clone.1), kind=kCustom, calls=%fused_computation.102 | custom fusion | flops 12800 | bytes 33792 | tf_op jit(solution)/shard_map/scatter-add | solution.py:134
  385.9 6.1 %scatter_fusion.1 = f32[20,416]{0,1:T(8,128)S(1)} fusion(f32[20,416]{0,1:T(8,128)S(1)} %scatter_custom_fusion.4, s32[640]{0:T(1024)S(1)} %fusion.41, f32[640,20]{1,0:T(8,128)S(1)} %copy.91), kind=kCustom, calls=%fused_computation.13 | custom fusion | flops 12800 | bytes 156160 | tf_op jit(solution)/shard_map/scatter-add | solution.py:134
  409.4 84.8 %all-reduce = (f32[]{:T(128)}, f32[]{:T(128)}) all-reduce(f32[]{:T(128)} %get-tuple-element.119, f32[]{:T(128)} %get-tuple-element.118), channel_id=1, replica_groups=mesh['sec'=64,'reg'=4] {'sec','reg'}, use_global_device_ids=true, to_apply=%region_7.10 | all-reduce | flops 2 | bytes 16 | tf_op jit(solution)/shard_map/psum | solution.py:139
  (400 shorter events, 295.1 us)
Async XLA Ops:
  1.4 12.7 %collective-permute-start = (f32[20,128]{0,1:T(8,128)S(1)}, f32[20,128]{0,1:T(8,128)S(1)}, u32[]{:S(2)}, u32[]{:S(2)}) collective-permute-start(f32[20,128]{0,1:T(8,128)S(1)} %bitcast.359), channel_id=1, source_target_pairs={{0,4},{4,8},{8,12},{12,16},{16,20},{20,24},{24,28},{28,32},{32,36}... | collective-permute-start | bytes 30728 | tf_op jit(solution)/shard_map/ppermute | solution.py:13
  7.8 12.7 %collective-permute-start.2 = (f32[1,20,16]{1,2,0:T(8,128)S(1)}, f32[1,20,16]{1,2,0:T(8,128)S(1)}, u32[]{:S(2)}, u32[]{:S(2)}) collective-permute-start(f32[1,20,16]{1,2,0:T(8,128)S(1)} %select_bitcast_fusion.7), channel_id=1, source_target_pairs={{0,1},{1,2},{2,3},{4,5},{5,6},{6,7},{8,9},{9,10},{10,11},{12,13},{... | collective-permute-start | bytes 3848 | tf_op jit(solution)/shard_map/ppermute | solution.py:23
  11.6 9.0 %collective-permute-start.3 = (f32[1,20,16]{1,2,0:T(8,128)S(1)}, f32[1,20,16]{1,2,0:T(8,128)S(1)}, u32[]{:S(2)}, u32[]{:S(2)}) collective-permute-start(f32[1,20,16]{1,2,0:T(8,128)S(1)} %select_bitcast_fusion.6), channel_id=1, source_target_pairs={{1,0},{2,1},{3,2},{5,4},{6,5},{7,6},{9,8},{10,9},{11,10},{13,12},{... | collective-permute-start | bytes 3848 | tf_op jit(solution)/shard_map/ppermute | solution.py:24
  14.2 6.5 %collective-permute-start.1 = (f32[20,128]{0,1:T(8,128)S(1)}, f32[20,128]{0,1:T(8,128)S(1)}, u32[]{:S(2)}, u32[]{:S(2)}) collective-permute-start(f32[20,128]{0,1:T(8,128)S(1)} %collective-permute-done), channel_id=1, source_target_pairs={{0,4},{4,8},{8,12},{12,16},{16,20},{20,24},{24,28},{28,32},{32,36}... | collective-permute-start | bytes 30728 | tf_op jit(solution)/shard_map/ppermute | solution.py:13
  175.0 27.8 %copy-start.3 = (f32[1,1,20,128]{2,3,1,0:T(8,128)S(1)}, f32[1,1,20,128]{2,3,1,0:T(8,128)}, u32[]{:S(2)}) copy-start(f32[1,1,20,128]{2,3,1,0:T(8,128)} %copy-done.2) | copy-start | bytes 30724
  175.9 36.4 %copy-start.13 = (pred[16]{0:T(512)(128)(4,1)S(1)}, pred[16]{0:T(512)(128)(4,1)}, u32[]{:S(2)}) copy-start(pred[16]{0:T(512)(128)(4,1)} %copy-done.12) | copy-start | bytes 52
  175.9 42.5 %copy-start.11 = (pred[16]{0:T(512)(128)(4,1)S(1)}, pred[16]{0:T(512)(128)(4,1)}, u32[]{:S(2)}) copy-start(pred[16]{0:T(512)(128)(4,1)} %copy-done.10) | copy-start | bytes 52
  189.7 5.6 %collective-permute-start.4 = (f32[20,128]{0,1:T(8,128)S(1)}, f32[20,128]{0,1:T(8,128)S(1)}, u32[]{:S(2)}, u32[]{:S(2)}) collective-permute-start(f32[20,128]{0,1:T(8,128)S(1)} %slice.106), channel_id=1, source_target_pairs={{4,0},{8,4},{12,8},{16,12},{20,16},{24,20},{28,24},{32,28},{36,32}... | collective-permute-start | bytes 30728 | tf_op jit(solution)/shard_map/ppermute | solution.py:13
  191.9 33.4 %copy-start.15 = (s32[16]{0:T(128)}, s32[16]{0:T(128)S(1)}, u32[]{:S(2)}) copy-start(s32[16]{0:T(128)S(1)} %get-tuple-element.210) | copy-start | bytes 196
  191.9 33.4 %copy-start.16 = (s32[16]{0:T(128)}, s32[16]{0:T(128)S(1)}, u32[]{:S(2)}) copy-start(s32[16]{0:T(128)S(1)} %get-tuple-element.211) | copy-start | bytes 196
  192.0 33.3 %copy-start.5 = (f32[1,1,20,128]{2,3,1,0:T(8,128)}, f32[1,1,20,128]{2,3,1,0:T(8,128)S(1)}, u32[]{:S(2)}) copy-start(f32[1,1,20,128]{2,3,1,0:T(8,128)S(1)} %copy.81) | copy-start | bytes 30724
  195.3 7.5 %collective-permute-start.5 = (f32[20,128]{0,1:T(8,128)S(1)}, f32[20,128]{0,1:T(8,128)S(1)}, u32[]{:S(2)}, u32[]{:S(2)}) collective-permute-start(f32[20,128]{0,1:T(8,128)S(1)} %slice_add_fusion.2), channel_id=1, source_target_pairs={{4,0},{8,4},{12,8},{16,12},{20,16},{24,20},{28,24},{32,28},{36,32}... | collective-permute-start | bytes 30728 | tf_op jit(solution)/shard_map/ppermute | solution.py:13
  197.2 5.6 %collective-permute-start.6 = (f32[1,20,16]{1,2,0:T(8,128)S(1)}, f32[1,20,16]{1,2,0:T(8,128)S(1)}, u32[]{:S(2)}, u32[]{:S(2)}) collective-permute-start(f32[1,20,16]{1,2,0:T(8,128)S(1)} %get-tuple-element.207), channel_id=1, source_target_pairs={{0,1},{1,2},{2,3},{4,5},{5,6},{6,7},{8,9},{9,10},{10,11},{12,13},{... | collective-permute-start | bytes 3848 | tf_op jit(solution)/shard_map/ppermute | solution.py:23
  201.5 4.4 collective-permute-start.7
  206.6 9.5 %collective-permute-start.8 = (f32[20,128]{0,1:T(8,128)S(1)}, f32[20,128]{0,1:T(8,128)S(1)}, u32[]{:S(2)}, u32[]{:S(2)}) collective-permute-start(f32[20,128]{0,1:T(8,128)S(1)} %bitcast_subtract_fusion), channel_id=1, source_target_pairs={{0,4},{4,8},{8,12},{12,16},{16,20},{20,24},{24,28},{28,32},{32,36}... | collective-permute-start | bytes 30728 | tf_op jit(solution)/shard_map/ppermute | solution.py:13
  213.0 6.8 %collective-permute-start.10 = (f32[1,20,16]{1,2,0:T(8,128)S(1)}, f32[1,20,16]{1,2,0:T(8,128)S(1)}, u32[]{:S(2)}, u32[]{:S(2)}) collective-permute-start(f32[1,20,16]{1,2,0:T(8,128)S(1)} %select_bitcast_fusion.5), channel_id=1, source_target_pairs={{0,1},{1,2},{2,3},{4,5},{5,6},{6,7},{8,9},{9,10},{10,11},{12,13},{... | collective-permute-start | bytes 3848 | tf_op jit(solution)/shard_map/ppermute | solution.py:23
  216.2 6.8 %collective-permute-start.9 = (f32[20,128]{0,1:T(8,128)S(1)}, f32[20,128]{0,1:T(8,128)S(1)}, u32[]{:S(2)}, u32[]{:S(2)}) collective-permute-start(f32[20,128]{0,1:T(8,128)S(1)} %collective-permute-done.8), channel_id=1, source_target_pairs={{0,4},{4,8},{8,12},{12,16},{16,20},{20,24},{24,28},{28,32},{32,36}... | collective-permute-start | bytes 30728 | tf_op jit(solution)/shard_map/ppermute | solution.py:13
  218.5 4.4 collective-permute-start.11
  377.3 27.6 %copy-start.6 = (f32[1,1,20,128]{2,3,1,0:T(8,128)S(1)}, f32[1,1,20,128]{2,3,1,0:T(8,128)}, u32[]{:S(2)}) copy-start(f32[1,1,20,128]{2,3,1,0:T(8,128)} %copy-done.5) | copy-start | bytes 30724
  377.3 118.3 %copy-start.4 = (f32[1,1,20,128]{2,3,1,0:T(8,128)S(1)}, f32[1,1,20,128]{2,3,1,0:T(8,128)}, u32[]{:S(2)}) copy-start(f32[1,1,20,128]{2,3,1,0:T(8,128)} %copy-done.2) | copy-start | bytes 30724
  392.0 6.8 %collective-permute-start.12 = (f32[20,128]{0,1:T(8,128)S(1)}, f32[20,128]{0,1:T(8,128)S(1)}, u32[]{:S(2)}, u32[]{:S(2)}) collective-permute-start(f32[20,128]{0,1:T(8,128)S(1)} %slice.111), channel_id=1, source_target_pairs={{4,0},{8,4},{12,8},{16,12},{20,16},{24,20},{28,24},{32,28},{36,32}... | collective-permute-start | bytes 30728 | tf_op jit(solution)/shard_map/ppermute | solution.py:13
  398.8 6.1 %collective-permute-start.13 = (f32[20,128]{0,1:T(8,128)S(1)}, f32[20,128]{0,1:T(8,128)S(1)}, u32[]{:S(2)}, u32[]{:S(2)}) collective-permute-start(f32[20,128]{0,1:T(8,128)S(1)} %slice_add_fusion), channel_id=1, source_target_pairs={{4,0},{8,4},{12,8},{16,12},{20,16},{24,20},{28,24},{32,28},{36,32}... | collective-permute-start | bytes 30728 | tf_op jit(solution)/shard_map/ppermute | solution.py:13
  400.8 4.2 collective-permute-start.14
  403.6 4.4 collective-permute-start.15
  (9 other events, 145.4 us)
where the time goes:
time: 506 us; the launch traced here: 497 us
  local copies, waits for them, and re-layouts  185 us (37%)
  matrix products  93.3 us (18%)
  blocking collectives  84.8 us (17%)
  other arithmetic  74.4 us (15%)
  starting transfers between devices  42.1 us (8%)
  waiting for transfers between devices  14.2 us (3%)
    another operation x20, local copies, waits for them, and re-layouts, monomials(): jnp.stack([constant, across, upward, square_a, mixed, square_b, square_a...  102 us
    psum x1, blocking collectives, global_dot(): return lax.psum(value, ('sec', 'reg'))  84.8 us
    dot_general x10, matrix products, block_terms(): jnp.einsum('mpk,cpk->cmp', basis_a, mismatch, precision=FULL_PRECISION)  34.1 us
    dot_general x10, matrix products, block_terms(): jnp.einsum('mpk,cmp->cpk', basis_a, own, precision=FULL_PRECISION)  27.9 us
    scatter-add x4, other arithmetic, apply_normal(): products = products.at[:, first].add(to_own).at[:, second].add(to_other)  25 us
    ppermute x8, starting transfers between devices, shifted(): return lax.ppermute(array, axis, pairs)  23.6 us
    mul x10, other arithmetic, monomials(): square_b * upward  19.2 us
    dot_general x10, matrix products, block_terms(): jnp.einsum('mpk,cpk->cmp', basis_b, mismatch, precision=FULL_PRECISION)  18.3 us
  transfers between devices with their start and end apart: 16, of which 5 were waited for; matrix products, arithmetic and copies ran while one was open for 2% of the time, Pallas kernels for 0%

commit v1 on v0

--- a/solution.py
+++ b/solution.py
@@ -136,7 +136,7 @@
 
 
 def global_dot(value):
-    return lax.psum(value, ("sec", "reg"))
+    return lax.psum(lax.psum(value, "reg"), "sec")
 
 
 def on_device(

time: 506 us -> 558 us (1.10)
  blocking collectives: 84.8 us -> 137 us
    psum x1 -> x2, blocking collectives: 84.8 us -> 137 us  [global_dot(): return lax.psum(lax.psum(value, 'reg'), 'sec')]
where the time goes in v1:
time: 558 us; the launch traced here: 549 us
  local copies, waits for them, and re-layouts  185 us (33%)
  blocking collectives  137 us (25%)
  matrix products  93.3 us (17%)
  other arithmetic  74.5 us (13%)
  starting transfers between devices  42.1 us (8%)
  waiting for transfers between devices  14.2 us (3%)
    psum x2, blocking collectives, global_dot(): return lax.psum(lax.psum(value, 'reg'), 'sec')  137 us
    another operation x20, local copies, waits for them, and re-layouts, monomials(): jnp.stack([constant, across, upward, square_a, mixed, square_b, square_a...  102 us
    dot_general x10, matrix products, block_terms(): jnp.einsum('mpk,cpk->cmp', basis_a, mismatch, precision=FULL_PRECISION)  34.1 us
    dot_general x10, matrix products, block_terms(): jnp.einsum('mpk,cmp->cpk', basis_a, own, precision=FULL_PRECISION)  27.9 us
    scatter-add x4, other arithmetic, apply_normal(): products = products.at[:, first].add(to_own).at[:, second].add(to_other)  25 us
    ppermute x8, starting transfers between devices, shifted(): return lax.ppermute(array, axis, pairs)  23.6 us
    mul x10, other arithmetic, monomials(): square_b * upward  19.3 us
    dot_general x10, matrix products, block_terms(): jnp.einsum('mpk,cpk->cmp', basis_b, mismatch, precision=FULL_PRECISION)  18.3 us
  transfers between devices with their start and end apart: 16, of which 5 were waited for; matrix products, arithmetic and copies ran while one was open for 2% of the time, Pallas kernels for 0%

profile of v1, /device:TPU:1, one launch (start us, length us, event | category | flops | bytes accessed | tf_op | source)
XLA Modules:
  0.0 548.8 jit_solution(2430020261831072376)
XLA Ops:
  1.4 4.9 collective-permute-start
  23.0 152.0 %while.24 = (s32[]{:T(128)}, f32[5,20,128]{2,1,0:T(8,128)}, f32[5,20,128]{2,1,0:T(8,128)}, s32[5,128]{1,0:T(8,128)S(1)}, f32[20,416]{0,1:T(8,128)}, /*index=5*/b...) while((s32[]{:T(128)}, f32[5,20,128]{2,1,0:T(8,128)}, ...), condition=%wide.region_1.4_spmd, body=%wide.region_0.3_spmd.sunk | while | flops 32287744 | bytes 16952436 | solution.py:128
  27.2 4.8 stack.53
  32.8 5.4 stack.52
  63.2 5.4 stack.52
  88.0 4.8 stack.53
  93.6 5.4 stack.52
  124.0 5.4 stack.52
  154.3 5.4 stack.52
  177.2 6.4 %scatter_custom_fusion = f32[20,416]{0,1:T(8,128)S(1)} fusion(s32[640]{0:T(1024)} %fusion.40, f32[640,20]{1,0:T(8,128)S(1)} %copy.78, f32[]{:T(128)} %constant.56.clone.1), kind=kCustom, calls=%fused_computation.104 | custom fusion | flops 12800 | bytes 33792 | tf_op jit(solution)/shard_map/scatter-add | solution.py:134
  183.6 6.1 %scatter_fusion = f32[20,416]{0,1:T(8,128)S(1)} fusion(f32[20,416]{0,1:T(8,128)S(1)} %scatter_custom_fusion, s32[640]{0:T(1024)S(1)} %fusion.41, f32[640,20]{1,0:T(8,128)S(1)} %copy.80), kind=kCustom, calls=%fused_computation.9 | custom fusion | flops 12800 | bytes 156160 | tf_op jit(solution)/shard_map/scatter-add | solution.py:134
  206.7 5.1 collective-permute-start.8
  225.3 152.0 %while.25 = (s32[]{:T(128)}, f32[5,20,128]{2,1,0:T(8,128)}, f32[5,20,128]{2,1,0:T(8,128)}, s32[5,128]{1,0:T(8,128)S(1)}, f32[20,416]{0,1:T(8,128)}, /*index=5*/b...) while((s32[]{:T(128)}, f32[5,20,128]{2,1,0:T(8,128)}, ...), condition=%wide.region_10.13_spmd, body=%wide.region_9.12_spmd.sunk | while | flops 32287744 | bytes 16952436 | solution.py:128
  235.1 5.4 stack.70
  259.9 4.8 stack.71
  265.5 5.4 stack.70
  290.3 4.8 stack.71
  295.9 5.4 stack.70
  326.3 5.4 stack.70
  356.7 5.4 stack.70
  379.5 6.4 %scatter_custom_fusion.4 = f32[20,416]{0,1:T(8,128)S(1)} fusion(s32[640]{0:T(1024)} %fusion.40, f32[640,20]{1,0:T(8,128)S(1)} %copy.89, f32[]{:T(128)} %constant.56.clone.1), kind=kCustom, calls=%fused_computation.102 | custom fusion | flops 12800 | bytes 33792 | tf_op jit(solution)/shard_map/scatter-add | solution.py:134
  385.9 6.1 %scatter_fusion.1 = f32[20,416]{0,1:T(8,128)S(1)} fusion(f32[20,416]{0,1:T(8,128)S(1)} %scatter_custom_fusion.4, s32[640]{0:T(1024)S(1)} %fusion.41, f32[640,20]{1,0:T(8,128)S(1)} %copy.91), kind=kCustom, calls=%fused_computation.13 | custom fusion | flops 12800 | bytes 156160 | tf_op jit(solution)/shard_map/scatter-add | solution.py:134
  409.5 6.8 %all-reduce.1 = (f32[]{:T(128)}, f32[]{:T(128)}) all-reduce(f32[]{:T(128)} %get-tuple-element.119, f32[]{:T(128)} %get-tuple-element.118), channel_id=1, replica_groups=mesh['sec'=64,'reg'=4] {'reg'}, use_global_device_ids=true, to_apply=%region_7.10 | all-reduce | flops 2 | bytes 16 | tf_op jit(solution)/shard_map/psum | solution.py:139
  416.2 129.8 %all-reduce = (f32[]{:T(128)}, f32[]{:T(128)}) all-reduce(f32[]{:T(128)} %get-tuple-element.154, f32[]{:T(128)} %get-tuple-element.155), channel_id=1, replica_groups=mesh['sec'=64,'reg'=4] {'sec'}, use_global_device_ids=true, to_apply=%region_8.11 | all-reduce | flops 2 | bytes 16 | tf_op jit(solution)/shard_map/psum | solution.py:139
  (401 shorter events, 300.0 us)
Async XLA Ops:
  1.4 12.7 %collective-permute-start = (f32[20,128]{0,1:T(8,128)S(1)}, f32[20,128]{0,1:T(8,128)S(1)}, u32[]{:S(2)}, u32[]{:S(2)}) collective-permute-start(f32[20,128]{0,1:T(8,128)S(1)} %bitcast.359), channel_id=1, source_target_pairs={{0,4},{4,8},{8,12},{12,16},{16,20},{20,24},{24,28},{28,32},{32,36}... | collective-permute-start | bytes 30728 | tf_op jit(solution)/shard_map/ppermute | solution.py:13
  7.8 12.7 %collective-permute-start.2 = (f32[1,20,16]{1,2,0:T(8,128)S(1)}, f32[1,20,16]{1,2,0:T(8,128)S(1)}, u32[]{:S(2)}, u32[]{:S(2)}) collective-permute-start(f32[1,20,16]{1,2,0:T(8,128)S(1)} %select_bitcast_fusion.7), channel_id=1, source_target_pairs={{0,1},{1,2},{2,3},{4,5},{5,6},{6,7},{8,9},{9,10},{10,11},{12,13},{... | collective-permute-start | bytes 3848 | tf_op jit(solution)/shard_map/ppermute | solution.py:23
  11.6 9.0 %collective-permute-start.3 = (f32[1,20,16]{1,2,0:T(8,128)S(1)}, f32[1,20,16]{1,2,0:T(8,128)S(1)}, u32[]{:S(2)}, u32[]{:S(2)}) collective-permute-start(f32[1,20,16]{1,2,0:T(8,128)S(1)} %select_bitcast_fusion.6), channel_id=1, source_target_pairs={{1,0},{2,1},{3,2},{5,4},{6,5},{7,6},{9,8},{10,9},{11,10},{13,12},{... | collective-permute-start | bytes 3848 | tf_op jit(solution)/shard_map/ppermute | solution.py:24
  14.2 6.5 %collective-permute-start.1 = (f32[20,128]{0,1:T(8,128)S(1)}, f32[20,128]{0,1:T(8,128)S(1)}, u32[]{:S(2)}, u32[]{:S(2)}) collective-permute-start(f32[20,128]{0,1:T(8,128)S(1)} %collective-permute-done), channel_id=1, source_target_pairs={{0,4},{4,8},{8,12},{12,16},{16,20},{20,24},{24,28},{28,32},{32,36}... | collective-permute-start | bytes 30728 | tf_op jit(solution)/shard_map/ppermute | solution.py:13
  175.0 27.8 %copy-start.3 = (f32[1,1,20,128]{2,3,1,0:T(8,128)S(1)}, f32[1,1,20,128]{2,3,1,0:T(8,128)}, u32[]{:S(2)}) copy-start(f32[1,1,20,128]{2,3,1,0:T(8,128)} %copy-done.2) | copy-start | bytes 30724
  175.9 36.4 %copy-start.13 = (pred[16]{0:T(512)(128)(4,1)S(1)}, pred[16]{0:T(512)(128)(4,1)}, u32[]{:S(2)}) copy-start(pred[16]{0:T(512)(128)(4,1)} %copy-done.12) | copy-start | bytes 52
  175.9 42.5 %copy-start.11 = (pred[16]{0:T(512)(128)(4,1)S(1)}, pred[16]{0:T(512)(128)(4,1)}, u32[]{:S(2)}) copy-start(pred[16]{0:T(512)(128)(4,1)} %copy-done.10) | copy-start | bytes 52
  189.7 5.6 %collective-permute-start.4 = (f32[20,128]{0,1:T(8,128)S(1)}, f32[20,128]{0,1:T(8,128)S(1)}, u32[]{:S(2)}, u32[]{:S(2)}) collective-permute-start(f32[20,128]{0,1:T(8,128)S(1)} %slice.106), channel_id=1, source_target_pairs={{4,0},{8,4},{12,8},{16,12},{20,16},{24,20},{28,24},{32,28},{36,32}... | collective-permute-start | bytes 30728 | tf_op jit(solution)/shard_map/ppermute | solution.py:13
  191.9 33.4 %copy-start.15 = (s32[16]{0:T(128)}, s32[16]{0:T(128)S(1)}, u32[]{:S(2)}) copy-start(s32[16]{0:T(128)S(1)} %get-tuple-element.212) | copy-start | bytes 196
  191.9 33.4 %copy-start.16 = (s32[16]{0:T(128)}, s32[16]{0:T(128)S(1)}, u32[]{:S(2)}) copy-start(s32[16]{0:T(128)S(1)} %get-tuple-element.213) | copy-start | bytes 196
  192.0 33.3 %copy-start.5 = (f32[1,1,20,128]{2,3,1,0:T(8,128)}, f32[1,1,20,128]{2,3,1,0:T(8,128)S(1)}, u32[]{:S(2)}) copy-start(f32[1,1,20,128]{2,3,1,0:T(8,128)S(1)} %copy.81) | copy-start | bytes 30724
  195.3 7.5 %collective-permute-start.5 = (f32[20,128]{0,1:T(8,128)S(1)}, f32[20,128]{0,1:T(8,128)S(1)}, u32[]{:S(2)}, u32[]{:S(2)}) collective-permute-start(f32[20,128]{0,1:T(8,128)S(1)} %slice_add_fusion.2), channel_id=1, source_target_pairs={{4,0},{8,4},{12,8},{16,12},{20,16},{24,20},{28,24},{32,28},{36,32}... | collective-permute-start | bytes 30728 | tf_op jit(solution)/shard_map/ppermute | solution.py:13
  197.3 5.6 %collective-permute-start.6 = (f32[1,20,16]{1,2,0:T(8,128)S(1)}, f32[1,20,16]{1,2,0:T(8,128)S(1)}, u32[]{:S(2)}, u32[]{:S(2)}) collective-permute-start(f32[1,20,16]{1,2,0:T(8,128)S(1)} %get-tuple-element.209), channel_id=1, source_target_pairs={{0,1},{1,2},{2,3},{4,5},{5,6},{6,7},{8,9},{9,10},{10,11},{12,13},{... | collective-permute-start | bytes 3848 | tf_op jit(solution)/shard_map/ppermute | solution.py:23
  201.5 4.4 collective-permute-start.7
  206.7 9.5 %collective-permute-start.8 = (f32[20,128]{0,1:T(8,128)S(1)}, f32[20,128]{0,1:T(8,128)S(1)}, u32[]{:S(2)}, u32[]{:S(2)}) collective-permute-start(f32[20,128]{0,1:T(8,128)S(1)} %bitcast_subtract_fusion), channel_id=1, source_target_pairs={{0,4},{4,8},{8,12},{12,16},{16,20},{20,24},{24,28},{28,32},{32,36}... | collective-permute-start | bytes 30728 | tf_op jit(solution)/shard_map/ppermute | solution.py:13
  213.1 6.8 %collective-permute-start.10 = (f32[1,20,16]{1,2,0:T(8,128)S(1)}, f32[1,20,16]{1,2,0:T(8,128)S(1)}, u32[]{:S(2)}, u32[]{:S(2)}) collective-permute-start(f32[1,20,16]{1,2,0:T(8,128)S(1)} %select_bitcast_fusion.5), channel_id=1, source_target_pairs={{0,1},{1,2},{2,3},{4,5},{5,6},{6,7},{8,9},{9,10},{10,11},{12,13},{... | collective-permute-start | bytes 3848 | tf_op jit(solution)/shard_map/ppermute | solution.py:23
  216.2 6.8 %collective-permute-start.9 = (f32[20,128]{0,1:T(8,128)S(1)}, f32[20,128]{0,1:T(8,128)S(1)}, u32[]{:S(2)}, u32[]{:S(2)}) collective-permute-start(f32[20,128]{0,1:T(8,128)S(1)} %collective-permute-done.8), channel_id=1, source_target_pairs={{0,4},{4,8},{8,12},{12,16},{16,20},{20,24},{24,28},{28,32},{32,36}... | collective-permute-start | bytes 30728 | tf_op jit(solution)/shard_map/ppermute | solution.py:13
  218.5 4.4 collective-permute-start.11
  377.3 27.6 %copy-start.6 = (f32[1,1,20,128]{2,3,1,0:T(8,128)S(1)}, f32[1,1,20,128]{2,3,1,0:T(8,128)}, u32[]{:S(2)}) copy-start(f32[1,1,20,128]{2,3,1,0:T(8,128)} %copy-done.5) | copy-start | bytes 30724
  377.3 170.0 %copy-start.4 = (f32[1,1,20,128]{2,3,1,0:T(8,128)S(1)}, f32[1,1,20,128]{2,3,1,0:T(8,128)}, u32[]{:S(2)}) copy-start(f32[1,1,20,128]{2,3,1,0:T(8,128)} %copy-done.2) | copy-start | bytes 30724
  392.1 6.8 %collective-permute-start.12 = (f32[20,128]{0,1:T(8,128)S(1)}, f32[20,128]{0,1:T(8,128)S(1)}, u32[]{:S(2)}, u32[]{:S(2)}) collective-permute-start(f32[20,128]{0,1:T(8,128)S(1)} %slice.111), channel_id=1, source_target_pairs={{4,0},{8,4},{12,8},{16,12},{20,16},{24,20},{28,24},{32,28},{36,32}... | collective-permute-start | bytes 30728 | tf_op jit(solution)/shard_map/ppermute | solution.py:13
  398.9 6.1 %collective-permute-start.13 = (f32[20,128]{0,1:T(8,128)S(1)}, f32[20,128]{0,1:T(8,128)S(1)}, u32[]{:S(2)}, u32[]{:S(2)}) collective-permute-start(f32[20,128]{0,1:T(8,128)S(1)} %slice_add_fusion), channel_id=1, source_target_pairs={{4,0},{8,4},{12,8},{16,12},{20,16},{24,20},{28,24},{32,28},{36,32}... | collective-permute-start | bytes 30728 | tf_op jit(solution)/shard_map/ppermute | solution.py:13
  400.8 4.2 collective-permute-start.14
  403.6 4.4 collective-permute-start.15
  (9 other events, 145.4 us)
